TPU v7x, 32 devices: a whole 2x2x4 slice. The times are simulated.
32 devices in a mesh: fac: 8 (over y, x, core), freq: 4 (over z).
Axes of the slice: x: 2, y: 2, z: 4, core: 2. Of those that a mesh axis runs over, the one named last changes fastest.
Arguments:
- right_side: float32 [16, 36864, 128], P('freq', 'fac'), may hold values from -6 to 6
- factors: bfloat16 [36864, 1024], P('fac'), may hold values from -0.03125 to 0.03125
- pair_weight: float32 [16, 36864], P('freq', 'fac'), may hold values from -2 to 2
- second_order: float32 [16, 36864], P('freq', 'fac'), may hold values from -1 to 1
- forward: float32 [16, 16], replicated, may hold values from -3 to 3
- backward: float32 [16, 16], replicated, may hold values from -3 to 3
Outputs:
- amplitude: float32 [16, 36864, 128], P('freq', 'fac')
- sources: float32 [16, 36864, 128], P('freq', 'fac')
All inputs are finite; a program needn't handle non-finite values.
Results may differ from a plain program's by a relative error of at most 0.0015.
Values may be sent and summed in bfloat16 or wider, within the bound.
A program may use at most 128 MiB of HBM per device.

v0:
```python
import jax
import jax.numpy as jnp
from jax import lax
from jax.sharding import PartitionSpec as P

OUTER = 2
INNER = 2


def shards(right_side, factors, pair_weight, second_order, forward, backward):
    weight = pair_weight[:, :, None]
    sources = right_side
    amplitude = sources
    for outer in range(OUTER):
        amplitude = sources
        for inner in range(INNER):
            rounded = amplitude.astype(jnp.bfloat16)
            partial_value = jnp.einsum(
                "pa,fpc->fac", factors, rounded, preferred_element_type=jnp.float32
            )
            projected = lax.psum(partial_value, "fac").astype(jnp.bfloat16)
            spread = jnp.einsum(
                "pa,fac->fpc", factors, projected, preferred_element_type=jnp.float32
            )
            amplitude = sources + weight * spread
        moved, kernel_rows = (
            lax.all_to_all(amplitude, "freq", split_axis=1, concat_axis=0, tiled=True),
            lax.all_to_all(second_order, "freq", split_axis=1, concat_axis=0, tiled=True),
        )
        timed = jnp.einsum("tw,wpc->tpc", forward, moved, precision=lax.Precision.HIGHEST)
        product = kernel_rows[:, :, None] * timed
        renewed = jnp.einsum("wt,tpc->wpc", backward, product, precision=lax.Precision.HIGHEST)
        returned = lax.all_to_all(renewed, "freq", split_axis=0, concat_axis=1, tiled=True)
        sources = right_side + returned
    return (amplitude, sources)


def solution(mesh):
    return jax.shard_map(
        shards,
        mesh=mesh,
        in_specs=(
            P("freq", "fac", None),
            P("fac", None),
            P("freq", "fac"),
            P("freq", "fac"),
            P(),
            P(),
        ),
        out_specs=(P("freq", "fac", None), P("freq", "fac", None)),
        check_vma=False,
    )
```

profile of v0, /device:TPU:3, one launch (start us, length us, event | category | flops | bytes accessed | tf_op | source)
XLA Modules:
  0.0 1309.2 jit_solution(18389353184218481441)
XLA Ops:
  14.8 10.4 fusion.42
  25.3 57.3 %all-reduce.4 = bf16[4,1024,128]{1,2,0:T(8,128)(2,1)S(1)} all-reduce(f32[4,1024,128]{1,2,0:T(8,128)S(1)} %fusion.42), channel_id=1, replica_groups=mesh['fac'=8,'freq'=4] {'fac'}, use_global_device_ids=true, to_apply=%region_0.0 | all-reduce | flops 524288 | bytes 3145728 | tf_op jit(solution)/shard_map/psum | solution.py:21
  82.5 19.6 %fusion.52 = f32[4,1024,128]{1,2,0:T(8,128)S(1)} fusion(bf16[4608,1024]{1,0:T(8,128)(2,1)} %param.7, f32[4,4608,128]{1,2,0:T(8,128)} %copy.50, f32[4,4608]{1,0:T(4,128)S(1)} %copy-done.4, bf16[4,1024,128]{1,2,0:T(8,128)(2,1)S(1)} %all-reduce.4), kind=kOutput, calls=%fused_computation.39 | convolution fusion | flops 9670754304 | bytes 22093824 | tf_op jit(solution)/shard_map/pa,fpc->fac/dot_general | solution.py:18
  102.1 56.3 %all-reduce.5 = bf16[4,1024,128]{1,2,0:T(8,128)(2,1)S(1)} all-reduce(f32[4,1024,128]{1,2,0:T(8,128)S(1)} %fusion.52), channel_id=1, replica_groups=mesh['fac'=8,'freq'=4] {'fac'}, use_global_device_ids=true, to_apply=%region_1.0 | all-reduce | flops 524288 | bytes 3145728 | tf_op jit(solution)/shard_map/psum | solution.py:21
  158.5 12.6 bitcast_add_fusion.3
  171.1 11.9 copy.44
  190.1 203.0 %all-to-all-done.1 = f32[4,4608,128]{2,0,1:T(4,128)} async-done(((f32[4,4608,128]{2,0,1:T(4,128)}), f32[4,4608,128]{2,0,1:T(4,128)}, u32[]{:S(2)}, u32[]{:S(2)}) %all-to-all-start.1) | async-done | bytes 9437216 | tf_op jit(solution)/shard_map/all_to_all | solution.py:27
  398.3 13.9 %fusion.22 = f32[1152,128,16]{1,2,0:T(8,128)S(1)} fusion(f32[16,1152,128]{2,1,0:T(8,128)S(1)} %bitcast.117, f32[16,16]{1,0:T(8,128)S(1)} %copy-done), kind=kOutput, calls=%fused_computation.29 | convolution fusion | flops 452984832 | bytes 18875392 | tf_op jit(solution)/shard_map/tw,wpc->tpc/dot_general | solution.py:30
  412.2 10.5 fusion.36
  425.8 210.0 %all_to_all.93 = f32[16,1152,128]{2,1,0:T(8,128)} all-to-all(f32[16,1152,128]{2,1,0:T(8,128)S(1)} %copy.48), channel_id=1, replica_groups=mesh['fac'=8,'freq'=4] {'freq'}, dimensions={0} | all-to-all | bytes 18874368 | tf_op jit(solution)/shard_map/all_to_all | solution.py:33
  635.7 11.9 copy.49
  647.6 11.3 all_to_all.79
  658.9 11.8 add.28
  670.7 10.3 fusion.47
  681.0 55.8 %all-reduce.6 = bf16[4,1024,128]{1,2,0:T(8,128)(2,1)S(1)} all-reduce(f32[4,1024,128]{1,2,0:T(8,128)S(1)} %fusion.47), channel_id=1, replica_groups=mesh['fac'=8,'freq'=4] {'fac'}, use_global_device_ids=true, to_apply=%region_2.0 | all-reduce | flops 524288 | bytes 3145728 | tf_op jit(solution)/shard_map/psum | solution.py:21
  736.8 19.6 %fusion.57 = f32[4,1024,128]{1,2,0:T(8,128)S(1)} fusion(bf16[4608,1024]{1,0:T(8,128)(2,1)} %param.7, f32[4,4608,128]{1,2,0:T(8,128)} %add.28, f32[4,4608]{1,0:T(4,128)S(1)} %copy-done.4, bf16[4,1024,128]{1,2,0:T(8,128)(2,1)S(1)} %all-reduce.6), kind=kOutput, calls=%fused_computation.40 | convolution fusion | flops 9670754304 | bytes 22093824 | tf_op jit(solution)/shard_map/pa,fpc->fac/dot_general | solution.py:18
  756.4 55.9 %all-reduce.7 = bf16[4,1024,128]{1,2,0:T(8,128)(2,1)S(1)} all-reduce(f32[4,1024,128]{1,2,0:T(8,128)S(1)} %fusion.57), channel_id=1, replica_groups=mesh['fac'=8,'freq'=4] {'fac'}, use_global_device_ids=true, to_apply=%region_3.0 | all-reduce | flops 524288 | bytes 3145728 | tf_op jit(solution)/shard_map/psum | solution.py:21
  812.3 12.6 bitcast_add_fusion.1
  825.0 11.8 copy.51
  836.8 208.6 %all_to_all.94 = f32[4,4608,128]{2,0,1:T(4,128)S(1)} all-to-all(f32[4,4608,128]{2,0,1:T(4,128)} %copy.51), channel_id=1, replica_groups=mesh['fac'=8,'freq'=4] {'freq'}, dimensions={1} | all-to-all | bytes 18874368 | tf_op jit(solution)/shard_map/all_to_all | solution.py:27
  1046.9 13.7 %fusion.20 = f32[1152,128,16]{1,2,0:T(8,128)S(1)} fusion(f32[16,1152,128]{2,1,0:T(8,128)S(1)} %bitcast.121, f32[16,16]{1,0:T(8,128)S(1)} %copy-done), kind=kOutput, calls=%fused_computation.27 | convolution fusion | flops 452984832 | bytes 18875392 | tf_op jit(solution)/shard_map/tw,wpc->tpc/dot_general | solution.py:30
  1060.6 10.5 fusion.37
  1093.0 196.4 %all-to-all-done.4 = f32[16,1152,128]{2,1,0:T(8,128)} async-done(((f32[16,1152,128]{2,1,0:T(8,128)}), f32[16,1152,128]{2,1,0:T(8,128)}, u32[]{:S(2)}, u32[]{:S(2)}) %all-to-all-start.4) | async-done | bytes 9437216 | tf_op jit(solution)/shard_map/all_to_all | solution.py:33
  1297.7 11.0 bitcast_add_fusion
  (25 shorter events, 61.2 us)
Async XLA Ops:
  0.6 397.7 %copy-start = (f32[16,16]{1,0:T(8,128)S(1)}, f32[16,16]{1,0:T(8,128)}, u32[]{:S(2)}) copy-start(f32[16,16]{1,0:T(8,128)} %param.10) | copy-start | bytes 3076
  0.6 182.3 %all-to-all-start = ((f32[4,4,1152]{2,0,1:T(4,128)}), f32[4,4,1152]{2,0,1:T(4,128)S(1)}, u32[]{:S(2)}, u32[]{:S(2)}) async-start(f32[4,4,1152]{2,0,1:T(4,128)} %bitcast.123), calls=%async_computation | async-start | bytes 147456 | tf_op jit(solution)/shard_map/all_to_all | solution.py:28
  14.8 67.7 %copy-start.4 = (f32[4,4608]{1,0:T(4,128)S(1)}, f32[4,4608]{1,0:T(4,128)}, u32[]{:S(2)}) copy-start(f32[4,4608]{1,0:T(4,128)} %param.8) | copy-start | bytes 221188
  183.0 210.1 %all-to-all-start.1 = ((f32[4,4608,128]{2,0,1:T(4,128)}), f32[4,4608,128]{2,0,1:T(4,128)}, u32[]{:S(2)}, u32[]{:S(2)}) async-start(f32[4,4608,128]{2,0,1:T(4,128)} %copy.44), calls=%async_computation.1 | async-start | bytes 18874368 | tf_op jit(solution)/shard_map/all_to_all | solution.py:27
  398.3 13.9 %copy-start.1 = (f32[16,1152]{0,1:T(8,128)S(1)}, f32[16,1152]{0,1:T(8,128)}, u32[]{:S(2)}) copy-start(f32[16,1152]{0,1:T(8,128)} %copy.40) | copy-start | bytes 221188
  398.3 13.9 %copy-start.3 = (f32[16,16]{1,0:T(8,128)S(1)}, f32[16,16]{1,0:T(8,128)}, u32[]{:S(2)}) copy-start(f32[16,16]{1,0:T(8,128)} %param.11) | copy-start | bytes 3076
  1046.8 13.8 %copy-start.2 = (f32[16,1152]{0,1:T(8,128)S(1)}, f32[16,1152]{0,1:T(8,128)}, u32[]{:S(2)}) copy-start(f32[16,1152]{0,1:T(8,128)} %copy.40) | copy-start | bytes 221188
  1077.6 211.8 %all-to-all-start.4 = ((f32[16,1152,128]{2,1,0:T(8,128)}), f32[16,1152,128]{2,1,0:T(8,128)}, u32[]{:S(2)}, u32[]{:S(2)}) async-start(f32[16,1152,128]{2,1,0:T(8,128)} %copy.55), calls=%async_computation.4 | async-start | bytes 18874368 | tf_op jit(solution)/shard_map/all_to_all | solution.py:33
where the time goes:
time: 1320 us; the launch traced here: 1310 us
  blocking collectives  644 us (49%)
  waiting for transfers between devices  399 us (30%)
  matrix products  134 us (10%)
  local copies, waits for them, and re-layouts  91.6 us (7%)
  other arithmetic  22.8 us (2%)
  starting transfers between devices  16.4 us (1%)
    psum x4, blocking collectives, shards(): projected = lax.psum(partial_value, 'fac').astype(jnp.bfloat16)  225 us
    all_to_all x1, blocking collectives, shards(): lax.all_to_all(renewed, 'freq', split_axis=0, concat_axis=1, tiled=True)  210 us
    all_to_all x1, blocking collectives, shards(): lax.all_to_all(amplitude, 'freq', split_axis=1, concat_axis=0, tiled=True)  209 us
    all_to_all x1, waiting for transfers between devices, shards(): lax.all_to_all(amplitude, 'freq', split_axis=1, concat_axis=0, tiled=True)  203 us
    all_to_all x1, waiting for transfers between devices, shards(): lax.all_to_all(renewed, 'freq', split_axis=0, concat_axis=1, tiled=True)  196 us
    dot_general x4, matrix products, shards(): jnp.einsum('pa,fpc->fac', factors, rounded, preferred_element_type=jnp.fl...  59.9 us
    all_to_all x3, local copies, waits for them, and re-layouts, shards(): lax.all_to_all(renewed, 'freq', split_axis=0, concat_axis=1, tiled=True)  31.4 us
    dot_general x2, matrix products, shards(): jnp.einsum('tw,wpc->tpc', forward, moved, precision=lax.Precision.HIGHEST)  27.6 us
  transfers between devices with their start and end apart: 3, of which 2 were waited for; matrix products, arithmetic and copies ran while one was open for 6% of the time, Pallas kernels for 0%

commit v1 on v0

--- a/solution.py
+++ b/solution.py
@@ -5,6 +5,12 @@
 
 OUTER = 2
 INNER = 2
+
+
+def summed_here(x, mesh_axis):
+    parts = lax.all_gather(x, mesh_axis, axis=0, tiled=False)
+    total = parts.sum(axis=0)
+    return total
 
 
 def shards(right_side, factors, pair_weight, second_order, forward, backward):
@@ -18,7 +24,7 @@
             partial_value = jnp.einsum(
                 "pa,fpc->fac", factors, rounded, preferred_element_type=jnp.float32
             )
-            projected = lax.psum(partial_value, "fac").astype(jnp.bfloat16)
+            projected = summed_here(partial_value, "fac").astype(jnp.bfloat16)
             spread = jnp.einsum(
                 "pa,fac->fpc", factors, projected, preferred_element_type=jnp.float32
             )

time: 1320 us -> 1490 us (1.13)
  waiting for transfers between devices: 399 us -> 746 us
  blocking collectives: 644 us -> 418 us
  other arithmetic: 22.8 us -> 50.2 us
    all_gather x0 -> x4, waiting for transfers between devices: none -> 346 us  [summed_here(): parts = lax.all_gather(x, mesh_axis, axis=0, tiled=False)]
    psum x4 -> x0, blocking collectives: 225 us -> none  [shards(): projected = lax.psum(partial_value, 'fac').astype(jnp.bfloat16)]
    reduce_sum x0 -> x4, other arithmetic: none -> 27.4 us  [summed_here(): total = parts.sum(axis=0)]
  transfers between devices with their start and end apart: 3 -> 7, of which waited for: 2 -> 6; matrix products, arithmetic and copies ran while one was open for 6% -> 4% of each run, Pallas kernels for 0% -> 0%
where the time goes in v1:
time: 1490 us; the launch traced here: 1480 us
  waiting for transfers between devices  746 us (50%)
  blocking collectives  418 us (28%)
  matrix products  134 us (9%)
  local copies, waits for them, and re-layouts  99.9 us (7%)
  other arithmetic  50.2 us (3%)
  starting transfers between devices  16.8 us (1%)
    all_gather x4, waiting for transfers between devices, summed_here(): parts = lax.all_gather(x, mesh_axis, axis=0, tiled=False)  346 us
    all_to_all x1, blocking collectives, shards(): lax.all_to_all(amplitude, 'freq', split_axis=1, concat_axis=0, tiled=True)  209 us
    all_to_all x1, blocking collectives, shards(): lax.all_to_all(renewed, 'freq', split_axis=0, concat_axis=1, tiled=True)  208 us
    all_to_all x1, waiting for transfers between devices, shards(): lax.all_to_all(amplitude, 'freq', split_axis=1, concat_axis=0, tiled=True)  204 us
    all_to_all x1, waiting for transfers between devices, shards(): lax.all_to_all(renewed, 'freq', split_axis=0, concat_axis=1, tiled=True)  196 us
    dot_general x4, matrix products, shards(): jnp.einsum('pa,fpc->fac', factors, rounded, preferred_element_type=jnp.fl...  59.7 us
    all_to_all x3, local copies, waits for them, and re-layouts, shards(): lax.all_to_all(renewed, 'freq', split_axis=0, concat_axis=1, tiled=True)  31.4 us
  transfers between devices with their start and end apart: 7, of which 6 were waited for; matrix products, arithmetic and copies ran while one was open for 4% of the time, Pallas kernels for 0%

profile of v1, /device:TPU:3, one launch (start us, length us, event | category | flops | bytes accessed | tf_op | source)
XLA Modules:
  0.0 1478.6 jit_solution(5861802933569559442)
XLA Ops:
  7.2 10.4 fusion.42
  29.2 81.8 %all-gather.9.cloned.1.call-done = f32[32,1024,128]{2,1,0:T(8,128)} async-done(((f32[4,1024,128]{2,1,0:T(8,128)}), f32[32,1024,128]{2,1,0:T(8,128)}) %all-gather.9.cloned.1.call-update) | async-done | bytes 16777232 | tf_op jit(solution)/shard_map/all_gather | solution.py:11
  118.4 19.5 %fusion.52 = f32[4,1024,128]{1,2,0:T(8,128)S(1)} fusion(bf16[4608,1024]{1,0:T(8,128)(2,1)} %param.7, f32[4,4608,128]{1,2,0:T(8,128)} %copy.87, f32[4,4608]{1,0:T(4,128)S(1)} %copy-done.4, bf16[4,1024,128]{1,2,0:T(8,128)(2,1)S(1)} %copy.102), kind=kOutput, calls=%fused_computation.39 | convolution fusion | flops 9670754304 | bytes 22093824 | tf_op jit(solution)/shard_map/pa,fpc->fac/dot_general | solution.py:24
  144.5 85.1 %all-gather.11.cloned.1.call-done = f32[32,1024,128]{2,1,0:T(8,128)} async-done(((f32[4,1024,128]{2,1,0:T(8,128)}), f32[32,1024,128]{2,1,0:T(8,128)}) %all-gather.11.cloned.1.call-update) | async-done | bytes 16777232 | tf_op jit(solution)/shard_map/all_gather | solution.py:11
  236.5 12.9 bitcast_add_fusion.3
  249.3 11.9 copy.81
  268.2 204.2 %all-to-all-done.1 = f32[4,4608,128]{2,0,1:T(4,128)} async-done(((f32[4,4608,128]{2,0,1:T(4,128)}), f32[4,4608,128]{2,0,1:T(4,128)}, u32[]{:S(2)}, u32[]{:S(2)}) %all-to-all-start.1) | async-done | bytes 9437216 | tf_op jit(solution)/shard_map/all_to_all | solution.py:33
  477.6 13.7 fusion.22
  491.3 10.5 fusion.36
  504.8 208.4 %all_to_all.93 = f32[16,1152,128]{2,1,0:T(8,128)} all-to-all(f32[16,1152,128]{2,1,0:T(8,128)S(1)} %copy.85), channel_id=1, replica_groups=mesh['fac'=8,'freq'=4] {'freq'}, dimensions={0} | all-to-all | bytes 18874368 | tf_op jit(solution)/shard_map/all_to_all | solution.py:39
  713.2 11.9 copy.86
  725.0 11.3 all_to_all.79
  736.3 11.8 add.20
  748.1 10.3 fusion.47
  760.6 89.4 %all-gather.13.cloned.1.call-done = f32[32,1024,128]{2,1,0:T(8,128)} async-done(((f32[4,1024,128]{2,1,0:T(8,128)}), f32[32,1024,128]{2,1,0:T(8,128)}) %all-gather.13.cloned.1.call-update) | async-done | bytes 16777232 | tf_op jit(solution)/shard_map/all_gather | solution.py:11
  857.4 19.5 %fusion.57 = f32[4,1024,128]{1,2,0:T(8,128)S(1)} fusion(bf16[4608,1024]{1,0:T(8,128)(2,1)} %param.7, f32[4,4608,128]{1,2,0:T(8,128)} %add.20, f32[4,4608]{1,0:T(4,128)S(1)} %copy-done.4, bf16[4,1024,128]{1,2,0:T(8,128)(2,1)S(1)} %copy.103), kind=kOutput, calls=%fused_computation.40 | convolution fusion | flops 9670754304 | bytes 22093824 | tf_op jit(solution)/shard_map/pa,fpc->fac/dot_general | solution.py:24
  878.7 89.9 %all-gather.15.cloned.1.call-done = f32[32,1024,128]{2,1,0:T(8,128)} async-done(((f32[4,1024,128]{2,1,0:T(8,128)}), f32[32,1024,128]{2,1,0:T(8,128)}) %all-gather.15.cloned.1.call-update) | async-done | bytes 16777232 | tf_op jit(solution)/shard_map/all_gather | solution.py:11
  975.4 12.9 bitcast_add_fusion.1
  988.3 11.8 copy.92
  1000.1 209.4 %all_to_all.94 = f32[4,4608,128]{2,0,1:T(4,128)S(1)} all-to-all(f32[4,4608,128]{2,0,1:T(4,128)} %copy.92), channel_id=1, replica_groups=mesh['fac'=8,'freq'=4] {'freq'}, dimensions={1} | all-to-all | bytes 18874368 | tf_op jit(solution)/shard_map/all_to_all | solution.py:33
  1211.0 13.7 fusion.20
  1224.7 10.5 fusion.37
  1257.1 195.5 %all-to-all-done.4 = f32[16,1152,128]{2,1,0:T(8,128)} async-done(((f32[16,1152,128]{2,1,0:T(8,128)}), f32[16,1152,128]{2,1,0:T(8,128)}, u32[]{:S(2)}, u32[]{:S(2)}) %all-to-all-start.4) | async-done | bytes 9437216 | tf_op jit(solution)/shard_map/all_to_all | solution.py:39
  1460.8 11.0 bitcast_add_fusion
  (43 shorter events, 97.3 us)
Async XLA Ops:
  7.2 470.4 %copy-start = (f32[16,16]{1,0:T(8,128)S(1)}, f32[16,16]{1,0:T(8,128)}, u32[]{:S(2)}) copy-start(f32[16,16]{1,0:T(8,128)} %param.10) | copy-start | bytes 3076
  7.2 103.8 %all-gather.9.cloned.1.call-start = ((), (), s32[]{:S(2)}) async-start(), calls=%async_computation.5 | async-start | bytes 18874368 | tf_op jit(solution)/shard_map/all_gather | solution.py:11
  19.5 210.1 %all-gather.11.cloned.1.call-start = ((), (), s32[]{:S(2)}) async-start(), calls=%async_computation.6 | async-start | bytes 18874368 | tf_op jit(solution)/shard_map/all_gather | solution.py:11
  111.0 7.4 copy-start.4
  139.7 121.5 %all-to-all-start = ((f32[4,4,1152]{2,0,1:T(4,128)}), f32[4,4,1152]{2,0,1:T(4,128)S(1)}, u32[]{:S(2)}, u32[]{:S(2)}) async-start(f32[4,4,1152]{2,0,1:T(4,128)} %bitcast), calls=%async_computation | async-start | bytes 147456 | tf_op jit(solution)/shard_map/all_to_all | solution.py:34
  261.2 211.2 %all-to-all-start.1 = ((f32[4,4608,128]{2,0,1:T(4,128)}), f32[4,4608,128]{2,0,1:T(4,128)}, u32[]{:S(2)}, u32[]{:S(2)}) async-start(f32[4,4608,128]{2,0,1:T(4,128)} %copy.81), calls=%async_computation.1 | async-start | bytes 18874368 | tf_op jit(solution)/shard_map/all_to_all | solution.py:33
  267.0 583.0 %all-gather.13.cloned.1.call-start = ((), (), s32[]{:S(2)}) async-start(), calls=%async_computation.7 | async-start | bytes 18874368 | tf_op jit(solution)/shard_map/all_gather | solution.py:11
  477.6 13.7 copy-start.1
  477.6 13.7 copy-start.3
  760.3 208.2 %all-gather.15.cloned.1.call-start = ((), (), s32[]{:S(2)}) async-start(), calls=%async_computation.8 | async-start | bytes 18874368 | tf_op jit(solution)/shard_map/all_gather | solution.py:11
  1211.0 13.7 copy-start.2
  1241.7 210.9 %all-to-all-start.4 = ((f32[16,1152,128]{2,1,0:T(8,128)}), f32[16,1152,128]{2,1,0:T(8,128)}, u32[]{:S(2)}, u32[]{:S(2)}) async-start(f32[16,1152,128]{2,1,0:T(8,128)} %copy.96), calls=%async_computation.4 | async-start | bytes 18874368 | tf_op jit(solution)/shard_map/all_to_all | solution.py:39
Sparse Core Ops, SparseCore 0:
  19.6 91.3 all-gather.8
  139.9 89.7 all-gather.10
  760.4 89.5 all-gather.12
  878.8 89.7 all-gather.14
